TPU v7x, 32 devices: a whole 2x2x4 slice. The times are simulated.
32 devices in a mesh: gx: 2 (over x), gy: 4 (over y, core), gz: 4 (over z).
Axes of the slice: x: 2, y: 2, z: 4, core: 2. Of those that a mesh axis runs over, the one named last changes fastest.
Arguments:
- solution_in: float32 [16, 128, 512], P('gx', 'gy', 'gz'), may hold values from -6 to 6
- residual_in: float32 [16, 128, 512], P('gx', 'gy', 'gz'), may hold values from -12 to 12
- direction_in: float32 [16, 128, 512], P('gx', 'gy', 'gz'), may hold values from -6 to 6
- material: int32 [16, 128, 512], P('gx', 'gy', 'gz'), may hold values from 0 to 7
- cond_table: float32 [8], replicated, may hold values from 0.5 to 4
- cap_table: float32 [8], replicated, may hold values from 0.2 to 1
- gas_flux: float32 [128, 512], P('gy', 'gz'), may hold values from -6 to 6
- supply_map: int32 [128, 512], P('gy', 'gz'), may hold values from 0 to 511, as said below
Outputs:
- solution: float32 [16, 128, 512], P('gx', 'gy', 'gz')
- residual: float32 [16, 128, 512], P('gx', 'gy', 'gz')
- direction: float32 [16, 128, 512], P('gx', 'gy', 'gz')
Inputs may be any that keep to these rules, and one draw needn't show every extreme that they name: `supply_map`: the gas faces are laid out so that the faces held by index q of gz, in their slots t * 128 / 4 to (t + 1) * 128 / 4 - 1, supply solid faces held by index t of gz in the same row; every gas face supplies exactly one solid face of its row.
All inputs are finite; a program needn't handle non-finite values.
Results may differ from a plain program's by a relative error of at most 0.0006.
Values sent between devices are 32-bit elements; how exact they have to be, the bound alone decides.
A program may use at most 64 MiB of HBM per device.

v0:
```python
import jax
import jax.numpy as jnp
from jax import lax
from jax.sharding import PartitionSpec as P

STEPS = 4


def extended(block, sides, width):
    for axis, dim in sides:
        count = lax.axis_size(axis)
        forward = [(i, i + 1) for i in range(count - 1)]
        backward = [(target, source) for source, target in forward]
        low = lax.ppermute(
            lax.slice_in_dim(block, block.shape[dim] - width, None, axis=dim), axis, forward
        )
        high = lax.ppermute(lax.slice_in_dim(block, 0, width, axis=dim), axis, backward)
        block = jnp.concatenate([low, block, high], axis=dim)
    return block


def harmonic(lower_side, upper_side):
    return (
        2.0
        * lower_side
        * upper_side
        / (jnp.where(lower_side > 0, lower_side, 1.0) + jnp.where(upper_side > 0, upper_side, 1.0))
    )


def face_terms(cond):
    return (
        harmonic(cond[:-1], cond[1:]),
        harmonic(cond[:, :-1], cond[:, 1:]),
        harmonic(cond[:, :, :-1], cond[:, :, 1:]),
    )


def operate(values, capacity, conductance):
    result = capacity * values
    face_flow = conductance[0] * (values[1:] - values[:-1])
    result = (
        result
        - jnp.pad(face_flow, ((0, 1), (0, 0), (0, 0)))
        + jnp.pad(face_flow, ((1, 0), (0, 0), (0, 0)))
    )
    face_flow = conductance[1] * (values[:, 1:] - values[:, :-1])
    result = (
        result
        - jnp.pad(face_flow, ((0, 0), (0, 1), (0, 0)))
        + jnp.pad(face_flow, ((0, 0), (1, 0), (0, 0)))
    )
    face_flow = conductance[2] * (values[:, :, 1:] - values[:, :, :-1])
    result = (
        result
        - jnp.pad(face_flow, ((0, 0), (0, 0), (0, 1)))
        + jnp.pad(face_flow, ((0, 0), (0, 0), (1, 0)))
    )
    return result


def lookup_code(codes, table):
    summed = jnp.zeros(codes.shape, jnp.float32)
    for material_id in range(table.shape[0]):
        summed = summed + jnp.where(
            codes == jnp.float32(material_id + 1), table[material_id], jnp.float32(0.0)
        )
    return summed


def spectrum(cond_table, cap_table):
    lowest = jnp.min(cap_table)
    highest = jnp.max(cap_table) + 12.0 * jnp.max(cond_table)
    return (0.5 * (highest + lowest), 0.5 * (highest - lowest))


def next_term(applied, terms, center, half_width):
    shifted = (applied - center * terms[-1]) / half_width
    if len(terms) == 1:
        return shifted
    return 2.0 * shifted - terms[-2]


def shift_matrix(center, half_width, steps):
    dimension = 2 * steps + 1
    matrix = jnp.zeros((dimension, dimension), jnp.float32)
    for offset, length in ((0, steps + 1), (steps + 1, steps)):
        for column in range(length - 1):
            matrix = matrix.at[offset + column, offset + column].set(center)
            matrix = matrix.at[offset + column + 1, offset + column].set(
                half_width if column == 0 else 0.5 * half_width
            )
            if column >= 1:
                matrix = matrix.at[offset + column - 1, offset + column].set(0.5 * half_width)
    return matrix


def coefficients(gram, center, half_width, steps):
    dimension = 2 * steps + 1
    matrix = shift_matrix(center, half_width, steps)
    highest_prec = lax.Precision.HIGHEST

    def gram_product(first_vec, second_vec):
        return jnp.dot(
            first_vec, jnp.dot(gram, second_vec, precision=highest_prec), precision=highest_prec
        )

    direct = jnp.zeros((dimension,), jnp.float32).at[0].set(1.0)
    residue = jnp.zeros((dimension,), jnp.float32).at[steps + 1].set(1.0)
    moved = jnp.zeros((dimension,), jnp.float32)
    norm_now = gram_product(residue, residue)
    for sweep in range(steps):
        mapped = jnp.dot(matrix, direct, precision=highest_prec)
        step_length = norm_now / gram_product(direct, mapped)
        moved = moved + step_length * direct
        residue = residue - step_length * mapped
        norm_next = gram_product(residue, residue)
        direct = residue + norm_next / norm_now * direct
        norm_now = norm_next
    return (moved, residue, direct)


def combine(weights, basis):
    summed = weights[0] * basis[0]
    for position in range(1, len(basis)):
        summed = summed + weights[position] * basis[position]
    return summed


def inside(values, depth):
    return values[depth:-depth, depth:-depth, depth:-depth]


def body(
    solution_in, residual_in, direction_in, material, cond_table, cap_table, gas_flux, supply_map
):
    surface_rows, surface_width = gas_flux.shape
    groups = lax.axis_size("gz")
    segment = surface_width // groups
    arrived = lax.all_to_all(
        gas_flux.reshape(surface_rows, groups, segment),
        "gz",
        split_axis=1,
        concat_axis=1,
        tiled=True,
    )
    arrived = arrived.reshape(surface_rows, surface_width)
    slot = (
        supply_map // surface_width * segment
        + supply_map % surface_width
        - lax.axis_index("gz") * segment
    )
    incoming = jnp.take_along_axis(arrived, slot, axis=1)
    is_top = lax.axis_index("gx") == lax.axis_size("gx") - 1
    start = residual_in.at[-1].add(jnp.where(is_top, incoming, jnp.float32(0.0)))
    codes = (material + 1).astype(jnp.float32)
    center, half_width = spectrum(cond_table, cap_table)
    first = extended(jnp.stack([direction_in, start, codes]), (("gx", 1), ("gy", 2), ("gz", 3)), 1)
    conductance = face_terms(lookup_code(first[2], cond_table))
    capacity_ext = lookup_code(first[2], cap_table)
    dir_terms = [direction_in]
    res_terms = [start]
    dir_applied = inside(operate(first[0], capacity_ext, conductance), 1)
    res_applied = inside(operate(first[1], capacity_ext, conductance), 1)
    res_terms.append(next_term(res_applied, res_terms, center, half_width))
    dir_terms.append(next_term(dir_applied, dir_terms, center, half_width))
    for sweep in range(1, STEPS):
        if sweep < STEPS - 1:
            layered = extended(
                jnp.stack([dir_terms[-1], res_terms[-1]]), (("gx", 1), ("gy", 2), ("gz", 3)), 1
            )
            dir_applied = inside(operate(layered[0], capacity_ext, conductance), 1)
            res_applied = inside(operate(layered[1], capacity_ext, conductance), 1)
            res_terms.append(next_term(res_applied, res_terms, center, half_width))
        else:
            layered = extended(dir_terms[-1], (("gx", 0), ("gy", 1), ("gz", 2)), 1)
            dir_applied = inside(operate(layered, capacity_ext, conductance), 1)
        dir_terms.append(next_term(dir_applied, dir_terms, center, half_width))
    basis = dir_terms + res_terms
    stacked = jnp.stack([term.reshape(-1) for term in basis])
    partial_gram = jnp.dot(stacked, stacked.T, precision=lax.Precision.HIGHEST)
    gram = lax.psum(partial_gram, ("gx", "gy", "gz"))
    moved, residue, direct = coefficients(gram, center, half_width, STEPS)
    return (solution_in + combine(moved, basis), combine(residue, basis), combine(direct, basis))


def solution(mesh):
    in_specs = (
        P("gx", "gy", "gz"),
        P("gx", "gy", "gz"),
        P("gx", "gy", "gz"),
        P("gx", "gy", "gz"),
        P(),
        P(),
        P("gy", "gz"),
        P("gy", "gz"),
    )
    out_specs = (P("gx", "gy", "gz"), P("gx", "gy", "gz"), P("gx", "gy", "gz"))
    return jax.shard_map(body, mesh=mesh, in_specs=in_specs, out_specs=out_specs, check_vma=False)
```

profile of v0, /device:TPU:0, one launch (start us, length us, event | category | flops | bytes accessed | tf_op | source)
XLA Modules:
  0.0 260.0 jit_solution(15775123754584945129)
XLA Ops:
  2.2 6.3 %all-to-all-start = ((f32[4,1,1024]{2,1,0:T(1,128)}), f32[4,1,1024]{2,1,0:T(1,128)S(1)}, u32[]{:S(2)}, u32[]{:S(2)}) async-start(f32[4,1,1024]{2,1,0:T(1,128)} %reshape.745), calls=%async_computation | async-start | bytes 32768 | tf_op jit(solution)/shard_map/all_to_all | solution.py:140
  10.2 3.9 %all-to-all-done = f32[4,1,1024]{2,1,0:T(1,128)S(1)} async-done(((f32[4,1,1024]{2,1,0:T(1,128)}), f32[4,1,1024]{2,1,0:T(1,128)S(1)}, u32[]{:S(2)}, u32[]{:S(2)}) %all-to-all-start) | async-done | bytes 16416 | tf_op jit(solution)/shard_map/all_to_all | solution.py:140
  15.6 25.6 %gather_fusion = f32[4096]{0:T(1024)S(1)} fusion(f32[32,128]{1,0:T(8,128)S(1)} %reshape.660, s32[4096]{0:T(1024)S(1)} %fusion.80), kind=kCustom, calls=%fused_computation | custom fusion | bytes 65536 | tf_op jit(solution)/shard_map/jit(take_along_axis)/gather | solution.py:153
  41.3 3.4 %collective-permute-start = (f32[3,1,32,128]{3,2,1,0:T(8,128)S(1)}, f32[3,1,32,128]{3,2,1,0:T(8,128)S(1)}, u32[]{:S(2)}, u32[]{:S(2)}) collective-permute-start(f32[3,1,32,128]{3,2,1,0:T(8,128)S(1)} %get-tuple-element.320), channel_id=1, source_target_pairs={{0,16},{1,17},{2,18},{3,19},{4,20},{5,21},{6,22},{7,23},{8,24},{9,... | collective-permute-start | bytes 147464 | tf_op jit(solution)/shard_map/ppermute | solution.py:14
  46.7 4.0 %collective-permute-done.1 = f32[3,1,32,128]{3,2,1,0:T(8,128)S(1)} collective-permute-done((f32[3,1,32,128]{3,2,1,0:T(8,128)S(1)}, f32[3,1,32,128]{3,2,1,0:T(8,128)S(1)}, u32[]{:S(2)}, u32[]{:S(2)}) %collective-permute-start.1) | collective-permute-done | bytes 49184 | tf_op jit(solution)/shard_map/ppermute | solution.py:17
  54.0 2.8 %collective-permute-done.3 = f32[3,10,1,128]{3,2,1,0:T(1,128)S(1)} collective-permute-done((f32[3,10,1,128]{3,2,1,0:T(1,128)S(1)}, f32[3,10,1,128]{3,2,1,0:T(1,128)S(1)}, u32[]{:S(2)}, u32[]{:S(2)}) %collective-permute-start.3) | collective-permute-done | bytes 15392 | tf_op jit(solution)/shard_map/ppermute | solution.py:17
  67.0 5.8 %bitcast_multiply_fusion.6 = (f32[10,34,130]{2,1,0:T(8,128)S(1)}, f32[1,10,34,130]{3,2,1,0:T(8,128)S(1)}, pred[1,10,34,130]{3,2,1,0:T(8,128)(4,1)S(1)}, pred[1,1...) fusion(f32[3,10,34,130]{3,2,1,0:T(8,128)S(1)} %pad_maximum_fusi, ...), kind=kLoop, calls=%fused_computation.85 | loop fusion | flops 1060800 | bytes 1060832 | tf_op jit(solution)/shard_map/mul | solution.py:40
  72.8 5.4 %add_add_fusion = f32[1,10,34,130]{3,2,1,0:T(8,128)S(1)} fusion(pred[1,10,34,130]{3,2,1,0:T(8,128)(4,1)S(1)} %get-tuple-element.283, pred[1,10,34,130]{3,2,1,0:T(8,128)(4,1)S(1)} %get-tuple-element.282, pred[1,10,34,130]{3,2,1,0:T(8,128)(4,1)S(1)} %get-tuple-element.281, pred[1,10,34,130]{3,2,1,0:T(8,128)(4,1)S(1)} %get-tuple-element.280, ...), kind=kLoop, calls=%fused_computation.86 | loop fusion | flops 663000 | bytes 530432 | tf_op jit(solution)/shard_map/add | solution.py:65
  82.8 4.2 %collective-permute-done.7 = f32[2,1,32,128]{3,2,1,0:T(8,128)S(1)} collective-permute-done((f32[2,1,32,128]{3,2,1,0:T(8,128)S(1)}, f32[2,1,32,128]{3,2,1,0:T(8,128)S(1)}, u32[]{:S(2)}, u32[]{:S(2)}) %collective-permute-start.7) | collective-permute-done | bytes 32800 | tf_op jit(solution)/shard_map/ppermute | solution.py:17
  90.8 3.3 %collective-permute-done.9 = f32[2,10,1,128]{3,2,1,0:T(1,128)S(1)} collective-permute-done((f32[2,10,1,128]{3,2,1,0:T(1,128)S(1)}, f32[2,10,1,128]{3,2,1,0:T(1,128)S(1)}, u32[]{:S(2)}, u32[]{:S(2)}) %collective-permute-start.9) | collective-permute-done | bytes 10272 | tf_op jit(solution)/shard_map/ppermute | solution.py:17
  94.3 4.3 %collective-permute-start.10 = (f32[2,10,34,1]{3,2,1,0:T(8,128)S(1)}, f32[2,10,34,1]{3,2,1,0:T(8,128)S(1)}, u32[]{:S(2)}, u32[]{:S(2)}) collective-permute-start(f32[2,10,34,1]{3,2,1,0:T(8,128)S(1)} %get-tuple-element.318), channel_id=1, source_target_pairs={{0,1},{1,2},{2,3},{4,5},{5,6},{6,7},{8,9},{9,10},{10,11},{12,13},{... | collective-permute-start | bytes 8168 | tf_op jit(solution)/shard_map/ppermute | solution.py:14
  99.9 7.0 %collective-permute-done.10 = f32[2,10,34,1]{3,2,1,0:T(8,128)S(1)} collective-permute-done((f32[2,10,34,1]{3,2,1,0:T(8,128)S(1)}, f32[2,10,34,1]{3,2,1,0:T(8,128)S(1)}, u32[]{:S(2)}, u32[]{:S(2)}) %collective-permute-start.10) | collective-permute-done | bytes 2752 | tf_op jit(solution)/shard_map/ppermute | solution.py:14
  106.9 4.7 %collective-permute-done.11 = f32[2,10,34,1]{3,2,1,0:T(8,128)S(1)} collective-permute-done((f32[2,10,34,1]{3,2,1,0:T(8,128)S(1)}, f32[2,10,34,1]{3,2,1,0:T(8,128)S(1)}, u32[]{:S(2)}, u32[]{:S(2)}) %collective-permute-start.11) | collective-permute-done | bytes 2752 | tf_op jit(solution)/shard_map/ppermute | solution.py:17
  116.7 4.2 %collective-permute-done.13 = f32[2,1,32,128]{3,2,1,0:T(8,128)S(1)} collective-permute-done((f32[2,1,32,128]{3,2,1,0:T(8,128)S(1)}, f32[2,1,32,128]{3,2,1,0:T(8,128)S(1)}, u32[]{:S(2)}, u32[]{:S(2)}) %collective-permute-start.13) | collective-permute-done | bytes 32800 | tf_op jit(solution)/shard_map/ppermute | solution.py:17
  129.9 7.0 %collective-permute-done.16 = f32[2,10,34,1]{3,2,1,0:T(8,128)S(1)} collective-permute-done((f32[2,10,34,1]{3,2,1,0:T(8,128)S(1)}, f32[2,10,34,1]{3,2,1,0:T(8,128)S(1)}, u32[]{:S(2)}, u32[]{:S(2)}) %collective-permute-start.16) | collective-permute-done | bytes 2752 | tf_op jit(solution)/shard_map/ppermute | solution.py:14
  136.9 4.7 %collective-permute-done.17 = f32[2,10,34,1]{3,2,1,0:T(8,128)S(1)} collective-permute-done((f32[2,10,34,1]{3,2,1,0:T(8,128)S(1)}, f32[2,10,34,1]{3,2,1,0:T(8,128)S(1)}, u32[]{:S(2)}, u32[]{:S(2)}) %collective-permute-start.17) | collective-permute-done | bytes 2752 | tf_op jit(solution)/shard_map/ppermute | solution.py:17
  147.5 4.2 %collective-permute-done.19 = f32[1,32,128]{2,1,0:T(8,128)S(1)} collective-permute-done((f32[1,32,128]{2,1,0:T(8,128)S(1)}, f32[1,32,128]{2,1,0:T(8,128)S(1)}, u32[]{:S(2)}, u32[]{:S(2)}) %collective-permute-start.19) | collective-permute-done | bytes 16416 | tf_op jit(solution)/shard_map/ppermute | solution.py:17
  167.0 3.3 %collective-permute-done.22 = f32[10,34,1]{2,1,0:T(8,128)S(1)} collective-permute-done((f32[10,34,1]{2,1,0:T(8,128)S(1)}, f32[10,34,1]{2,1,0:T(8,128)S(1)}, u32[]{:S(2)}, u32[]{:S(2)}) %collective-permute-start.22) | collective-permute-done | bytes 1392 | tf_op jit(solution)/shard_map/ppermute | solution.py:14
  170.3 4.7 %collective-permute-done.23 = f32[10,34,1]{2,1,0:T(8,128)S(1)} collective-permute-done((f32[10,34,1]{2,1,0:T(8,128)S(1)}, f32[10,34,1]{2,1,0:T(8,128)S(1)}, u32[]{:S(2)}, u32[]{:S(2)}) %collective-permute-start.23) | collective-permute-done | bytes 1392 | tf_op jit(solution)/shard_map/ppermute | solution.py:17
  180.0 2.9 %fusion.119 = f32[9,9]{1,0:T(8,128)S(1)} fusion(f32[9,32768]{1,0:T(8,128)S(1)} %stack.43), kind=kOutput, calls=%fused_computation.275 | convolution fusion | flops 31850496 | bytes 1179972 | tf_op jit(solution)/shard_map/dot_general | solution.py:181
  183.0 38.1 %psum.7 = f32[9,9]{1,0:T(8,128)S(1)} all-reduce(f32[9,9]{1,0:T(8,128)S(1)} %fusion.119), channel_id=1, replica_groups=mesh['gx'=2,'gy'=4,'gz'=4] {'gx','gy','gz'}, use_global_device_ids=true, to_apply=%region_3.4 | all-reduce | flops 81 | bytes 648 | tf_op jit(solution)/shard_map/psum | solution.py:182
  240.9 6.2 %multiply_add_fusion = f32[8,32,128]{2,1,0:T(8,128)} fusion(f32[8,32,128]{2,1,0:T(8,128)S(1)} %fusion.54, f32[8,32,128]{2,1,0:T(8,128)S(1)} %fusion.66, f32[8,32,128]{2,1,0:T(8,128)S(1)} %get-tuple-element.383, f32[8,32,128]{2,1,0:T(8,128)S(1)} %fusion.78, f32[8,32,128]{2,1,0:T(8,128)S(1)} %fusion.58, f32[8,32,128]{2,1,0:T(8,128)S(1)} %fusion.62, ...), kind=kLoop, calls=%fused_computation.187 | loop fusion | flops 557056 | bytes 1310756 | tf_op jit(solution)/shard_map/add | solution.py:126
  247.2 6.4 %multiply_add_fusion.1 = f32[8,32,128]{2,1,0:T(8,128)} fusion(f32[8,32,128]{2,1,0:T(8,128)S(1)} %fusion.54, f32[8,32,128]{2,1,0:T(8,128)S(1)} %fusion.66, f32[8,32,128]{2,1,0:T(8,128)S(1)} %get-tuple-element.383, f32[8,32,128]{2,1,0:T(8,128)S(1)} %fusion.78, f32[8,32,128]{2,1,0:T(8,128)S(1)} %fusion.58, f32[8,32,128]{2,1,0:T(8,128)S(1)} %fusion.62, ...), kind=kLoop, calls=%fused_computation.188 | loop fusion | flops 557056 | bytes 1310756 | tf_op jit(solution)/shard_map/add | solution.py:126
  253.6 6.4 %add_add_fusion.2 = f32[8,32,128]{2,1,0:T(8,128)} fusion(f32[8,32,128]{2,1,0:T(8,128)S(1)} %copy-done.3, f32[8,32,128]{2,1,0:T(8,128)S(1)} %fusion.54, f32[8,32,128]{2,1,0:T(8,128)S(1)} %fusion.66, f32[8,32,128]{2,1,0:T(8,128)S(1)} %get-tuple-element.383, f32[8,32,128]{2,1,0:T(8,128)S(1)} %fusion.78, f32[8,32,128]{2,1,0:T(8,128)S(1)} %fusion.58, ...), kind=kLoop, calls=%fused_computation.189 | loop fusion | flops 589824 | bytes 1441828 | tf_op jit(solution)/shard_map/add | solution.py:184
  (169 shorter events, 75.0 us)
Async XLA Ops:
  2.2 11.9 %all-to-all-start = ((f32[4,1,1024]{2,1,0:T(1,128)}), f32[4,1,1024]{2,1,0:T(1,128)S(1)}, u32[]{:S(2)}, u32[]{:S(2)}) async-start(f32[4,1,1024]{2,1,0:T(1,128)} %reshape.745), calls=%async_computation | async-start | bytes 32768 | tf_op jit(solution)/shard_map/all_to_all | solution.py:140
  41.3 5.4 %collective-permute-start = (f32[3,1,32,128]{3,2,1,0:T(8,128)S(1)}, f32[3,1,32,128]{3,2,1,0:T(8,128)S(1)}, u32[]{:S(2)}, u32[]{:S(2)}) collective-permute-start(f32[3,1,32,128]{3,2,1,0:T(8,128)S(1)} %get-tuple-element.320), channel_id=1, source_target_pairs={{0,16},{1,17},{2,18},{3,19},{4,20},{5,21},{6,22},{7,23},{8,24},{9,... | collective-permute-start | bytes 147464 | tf_op jit(solution)/shard_map/ppermute | solution.py:14
  44.7 6.0 %collective-permute-start.1 = (f32[3,1,32,128]{3,2,1,0:T(8,128)S(1)}, f32[3,1,32,128]{3,2,1,0:T(8,128)S(1)}, u32[]{:S(2)}, u32[]{:S(2)}) collective-permute-start(f32[3,1,32,128]{3,2,1,0:T(8,128)S(1)} %get-tuple-element.321), channel_id=1, source_target_pairs={{16,0},{17,1},{18,2},{19,3},{20,4},{21,5},{22,6},{23,7},{24,8},{25... | collective-permute-start | bytes 147464 | tf_op jit(solution)/shard_map/ppermute | solution.py:17
  50.7 3.3 %collective-permute-start.2 = (f32[3,10,1,128]{3,2,1,0:T(1,128)S(1)}, f32[3,10,1,128]{3,2,1,0:T(1,128)S(1)}, u32[]{:S(2)}, u32[]{:S(2)}) collective-permute-start(f32[3,10,1,128]{3,2,1,0:T(1,128)S(1)} %get-tuple-element.306), channel_id=1, source_target_pairs={{0,4},{4,8},{8,12},{1,5},{5,9},{9,13},{2,6},{6,10},{10,14},{3,7},{... | collective-permute-start | bytes 46088 | tf_op jit(solution)/shard_map/ppermute | solution.py:14
  52.0 4.8 %collective-permute-start.3 = (f32[3,10,1,128]{3,2,1,0:T(1,128)S(1)}, f32[3,10,1,128]{3,2,1,0:T(1,128)S(1)}, u32[]{:S(2)}, u32[]{:S(2)}) collective-permute-start(f32[3,10,1,128]{3,2,1,0:T(1,128)S(1)} %get-tuple-element.307), channel_id=1, source_target_pairs={{4,0},{8,4},{12,8},{5,1},{9,5},{13,9},{6,2},{10,6},{14,10},{7,3},{... | collective-permute-start | bytes 46088 | tf_op jit(solution)/shard_map/ppermute | solution.py:17
  57.4 7.8 %collective-permute-start.4 = (f32[3,10,34,1]{2,3,1,0:T(1,128)S(1)}, f32[3,10,34,1]{2,3,1,0:T(1,128)S(1)}, u32[]{:S(2)}, u32[]{:S(2)}) collective-permute-start(f32[3,10,34,1]{2,3,1,0:T(1,128)S(1)} %copy.31), channel_id=1, source_target_pairs={{0,1},{1,2},{2,3},{4,5},{5,6},{6,7},{8,9},{9,10},{10,11},{12,13},{... | collective-permute-start | bytes 12248 | tf_op jit(solution)/shard_map/ppermute | solution.py:14
  60.3 5.6 %collective-permute-start.5 = (f32[3,10,34,1]{2,3,1,0:T(1,128)S(1)}, f32[3,10,34,1]{2,3,1,0:T(1,128)S(1)}, u32[]{:S(2)}, u32[]{:S(2)}) collective-permute-start(f32[3,10,34,1]{2,3,1,0:T(1,128)S(1)} %copy.32), channel_id=1, source_target_pairs={{1,0},{2,1},{3,2},{5,4},{6,5},{7,6},{9,8},{10,9},{11,10},{13,12},{... | collective-permute-start | bytes 12248 | tf_op jit(solution)/shard_map/ppermute | solution.py:17
  79.7 3.2 %collective-permute-start.6 = (f32[2,1,32,128]{3,2,1,0:T(8,128)S(1)}, f32[2,1,32,128]{3,2,1,0:T(8,128)S(1)}, u32[]{:S(2)}, u32[]{:S(2)}) collective-permute-start(f32[2,1,32,128]{3,2,1,0:T(8,128)S(1)} %get-tuple-element.328), channel_id=1, source_target_pairs={{0,16},{1,17},{2,18},{3,19},{4,20},{5,21},{6,22},{7,23},{8,24},{9,... | collective-permute-start | bytes 98312 | tf_op jit(solution)/shard_map/ppermute | solution.py:14
  81.3 5.8 %collective-permute-start.7 = (f32[2,1,32,128]{3,2,1,0:T(8,128)S(1)}, f32[2,1,32,128]{3,2,1,0:T(8,128)S(1)}, u32[]{:S(2)}, u32[]{:S(2)}) collective-permute-start(f32[2,1,32,128]{3,2,1,0:T(8,128)S(1)} %get-tuple-element.329), channel_id=1, source_target_pairs={{16,0},{17,1},{18,2},{19,3},{20,4},{21,5},{22,6},{23,7},{24,8},{25... | collective-permute-start | bytes 98312 | tf_op jit(solution)/shard_map/ppermute | solution.py:17
  87.1 3.7 %collective-permute-start.8 = (f32[2,10,1,128]{3,2,1,0:T(1,128)S(1)}, f32[2,10,1,128]{3,2,1,0:T(1,128)S(1)}, u32[]{:S(2)}, u32[]{:S(2)}) collective-permute-start(f32[2,10,1,128]{3,2,1,0:T(1,128)S(1)} %get-tuple-element.324), channel_id=1, source_target_pairs={{0,4},{4,8},{8,12},{1,5},{5,9},{9,13},{2,6},{6,10},{10,14},{3,7},{... | collective-permute-start | bytes 30728 | tf_op jit(solution)/shard_map/ppermute | solution.py:14
  89.5 4.6 %collective-permute-start.9 = (f32[2,10,1,128]{3,2,1,0:T(1,128)S(1)}, f32[2,10,1,128]{3,2,1,0:T(1,128)S(1)}, u32[]{:S(2)}, u32[]{:S(2)}) collective-permute-start(f32[2,10,1,128]{3,2,1,0:T(1,128)S(1)} %get-tuple-element.325), channel_id=1, source_target_pairs={{4,0},{8,4},{12,8},{5,1},{9,5},{13,9},{6,2},{10,6},{14,10},{7,3},{... | collective-permute-start | bytes 30728 | tf_op jit(solution)/shard_map/ppermute | solution.py:17
  94.3 12.6 %collective-permute-start.10 = (f32[2,10,34,1]{3,2,1,0:T(8,128)S(1)}, f32[2,10,34,1]{3,2,1,0:T(8,128)S(1)}, u32[]{:S(2)}, u32[]{:S(2)}) collective-permute-start(f32[2,10,34,1]{3,2,1,0:T(8,128)S(1)} %get-tuple-element.318), channel_id=1, source_target_pairs={{0,1},{1,2},{2,3},{4,5},{5,6},{6,7},{8,9},{9,10},{10,11},{12,13},{... | collective-permute-start | bytes 8168 | tf_op jit(solution)/shard_map/ppermute | solution.py:14
  98.6 13.0 %collective-permute-start.11 = (f32[2,10,34,1]{3,2,1,0:T(8,128)S(1)}, f32[2,10,34,1]{3,2,1,0:T(8,128)S(1)}, u32[]{:S(2)}, u32[]{:S(2)}) collective-permute-start(f32[2,10,34,1]{3,2,1,0:T(8,128)S(1)} %get-tuple-element.319), channel_id=1, source_target_pairs={{1,0},{2,1},{3,2},{5,4},{6,5},{7,6},{9,8},{10,9},{11,10},{13,12},{... | collective-permute-start | bytes 8168 | tf_op jit(solution)/shard_map/ppermute | solution.py:17
  113.4 3.3 %collective-permute-start.12 = (f32[2,1,32,128]{3,2,1,0:T(8,128)S(1)}, f32[2,1,32,128]{3,2,1,0:T(8,128)S(1)}, u32[]{:S(2)}, u32[]{:S(2)}) collective-permute-start(f32[2,1,32,128]{3,2,1,0:T(8,128)S(1)} %get-tuple-element.326), channel_id=1, source_target_pairs={{0,16},{1,17},{2,18},{3,19},{4,20},{5,21},{6,22},{7,23},{8,24},{9,... | collective-permute-start | bytes 98312 | tf_op jit(solution)/shard_map/ppermute | solution.py:14
  115.0 5.9 %collective-permute-start.13 = (f32[2,1,32,128]{3,2,1,0:T(8,128)S(1)}, f32[2,1,32,128]{3,2,1,0:T(8,128)S(1)}, u32[]{:S(2)}, u32[]{:S(2)}) collective-permute-start(f32[2,1,32,128]{3,2,1,0:T(8,128)S(1)} %get-tuple-element.327), channel_id=1, source_target_pairs={{16,0},{17,1},{18,2},{19,3},{20,4},{21,5},{22,6},{23,7},{24,8},{25... | collective-permute-start | bytes 98312 | tf_op jit(solution)/shard_map/ppermute | solution.py:17
  120.9 3.1 %collective-permute-start.14 = (f32[2,10,1,128]{3,2,1,0:T(1,128)S(1)}, f32[2,10,1,128]{3,2,1,0:T(1,128)S(1)}, u32[]{:S(2)}, u32[]{:S(2)}) collective-permute-start(f32[2,10,1,128]{3,2,1,0:T(1,128)S(1)} %get-tuple-element.322), channel_id=1, source_target_pairs={{0,4},{4,8},{8,12},{1,5},{5,9},{9,13},{2,6},{6,10},{10,14},{3,7},{... | collective-permute-start | bytes 30728 | tf_op jit(solution)/shard_map/ppermute | solution.py:14
  122.7 3.2 %collective-permute-start.15 = (f32[2,10,1,128]{3,2,1,0:T(1,128)S(1)}, f32[2,10,1,128]{3,2,1,0:T(1,128)S(1)}, u32[]{:S(2)}, u32[]{:S(2)}) collective-permute-start(f32[2,10,1,128]{3,2,1,0:T(1,128)S(1)} %get-tuple-element.323), channel_id=1, source_target_pairs={{4,0},{8,4},{12,8},{5,1},{9,5},{13,9},{6,2},{10,6},{14,10},{7,3},{... | collective-permute-start | bytes 30728 | tf_op jit(solution)/shard_map/ppermute | solution.py:17
  126.2 10.7 %collective-permute-start.16 = (f32[2,10,34,1]{3,2,1,0:T(8,128)S(1)}, f32[2,10,34,1]{3,2,1,0:T(8,128)S(1)}, u32[]{:S(2)}, u32[]{:S(2)}) collective-permute-start(f32[2,10,34,1]{3,2,1,0:T(8,128)S(1)} %get-tuple-element.312), channel_id=1, source_target_pairs={{0,1},{1,2},{2,3},{4,5},{5,6},{6,7},{8,9},{9,10},{10,11},{12,13},{... | collective-permute-start | bytes 8168 | tf_op jit(solution)/shard_map/ppermute | solution.py:14
  128.6 13.0 %collective-permute-start.17 = (f32[2,10,34,1]{3,2,1,0:T(8,128)S(1)}, f32[2,10,34,1]{3,2,1,0:T(8,128)S(1)}, u32[]{:S(2)}, u32[]{:S(2)}) collective-permute-start(f32[2,10,34,1]{3,2,1,0:T(8,128)S(1)} %get-tuple-element.313), channel_id=1, source_target_pairs={{1,0},{2,1},{3,2},{5,4},{6,5},{7,6},{9,8},{10,9},{11,10},{13,12},{... | collective-permute-start | bytes 8168 | tf_op jit(solution)/shard_map/ppermute | solution.py:17
  146.1 5.6 %collective-permute-start.19 = (f32[1,32,128]{2,1,0:T(8,128)S(1)}, f32[1,32,128]{2,1,0:T(8,128)S(1)}, u32[]{:S(2)}, u32[]{:S(2)}) collective-permute-start(f32[1,32,128]{2,1,0:T(8,128)S(1)} %get-tuple-element.335), channel_id=1, source_target_pairs={{16,0},{17,1},{18,2},{19,3},{20,4},{21,5},{22,6},{23,7},{24,8},{25... | collective-permute-start | bytes 49160 | tf_op jit(solution)/shard_map/ppermute | solution.py:17
  151.7 11.2 %collective-permute-start.20 = (f32[10,1,128]{2,1,0:T(1,128)S(1)}, f32[10,1,128]{2,1,0:T(1,128)S(1)}, u32[]{:S(2)}, u32[]{:S(2)}) collective-permute-start(f32[10,1,128]{2,1,0:T(1,128)S(1)} %get-tuple-element.332), channel_id=1, source_target_pairs={{0,4},{4,8},{8,12},{1,5},{5,9},{9,13},{2,6},{6,10},{10,14},{3,7},{... | collective-permute-start | bytes 15368 | tf_op jit(solution)/shard_map/ppermute | solution.py:14
  153.2 9.7 %collective-permute-start.21 = (f32[10,1,128]{2,1,0:T(1,128)S(1)}, f32[10,1,128]{2,1,0:T(1,128)S(1)}, u32[]{:S(2)}, u32[]{:S(2)}) collective-permute-start(f32[10,1,128]{2,1,0:T(1,128)S(1)} %get-tuple-element.333), channel_id=1, source_target_pairs={{4,0},{8,4},{12,8},{5,1},{9,5},{13,9},{6,2},{10,6},{14,10},{7,3},{... | collective-permute-start | bytes 15368 | tf_op jit(solution)/shard_map/ppermute | solution.py:17
  163.1 7.2 %collective-permute-start.22 = (f32[10,34,1]{2,1,0:T(8,128)S(1)}, f32[10,34,1]{2,1,0:T(8,128)S(1)}, u32[]{:S(2)}, u32[]{:S(2)}) collective-permute-start(f32[10,34,1]{2,1,0:T(8,128)S(1)} %get-tuple-element.330), channel_id=1, source_target_pairs={{0,1},{1,2},{2,3},{4,5},{5,6},{6,7},{8,9},{9,10},{10,11},{12,13},{... | collective-permute-start | bytes 4088 | tf_op jit(solution)/shard_map/ppermute | solution.py:14
  165.6 9.5 %collective-permute-start.23 = (f32[10,34,1]{2,1,0:T(8,128)S(1)}, f32[10,34,1]{2,1,0:T(8,128)S(1)}, u32[]{:S(2)}, u32[]{:S(2)}) collective-permute-start(f32[10,34,1]{2,1,0:T(8,128)S(1)} %get-tuple-element.331), channel_id=1, source_target_pairs={{1,0},{2,1},{3,2},{5,4},{6,5},{7,6},{9,8},{10,9},{11,10},{13,12},{... | collective-permute-start | bytes 4088 | tf_op jit(solution)/shard_map/ppermute | solution.py:17
  (12 other events, 309.3 us)
where the time goes:
time: 262 us; the launch traced here: 260 us
  waiting for transfers between devices  61.3 us (23%)
  starting transfers between devices  48.7 us (19%)
  other arithmetic  43.5 us (17%)
  local copies, waits for them, and re-layouts  42.3 us (16%)
  blocking collectives  38.1 us (15%)
  between operations  15.9 us (6%)
  matrix products  10.1 us (4%)
    ppermute x12, waiting for transfers between devices, extended(): lax.ppermute(lax.slice_in_dim(block, 0, width, axis=dim), axis, backward)  39.2 us
    psum x1, blocking collectives, body(): gram = lax.psum(partial_gram, ('gx', 'gy', 'gz'))  38.1 us
    ppermute x12, starting transfers between devices, extended(): lax.ppermute(lax.slice_in_dim(block, block.shape[dim] - width, None, axis...  26.8 us
    gather x1, local copies, waits for them, and re-layouts, body(): incoming = jnp.take_along_axis(arrived, slot, axis=1)  25.6 us
    ppermute x12, waiting for transfers between devices, extended(): lax.ppermute(lax.slice_in_dim(block, block.shape[dim] - width, None, axis...  18.2 us
    ppermute x12, starting transfers between devices, extended(): lax.ppermute(lax.slice_in_dim(block, 0, width, axis=dim), axis, backward)  15.5 us
    add x2, other arithmetic, combine(): summed = summed + weights[position] * basis[position]  12.6 us
    mul x5, other arithmetic, operate(): result = capacity * values  7.02 us
  transfers between devices with their start and end apart: 25, of which 18 were waited for; matrix products, arithmetic and copies ran while one was open for 5% of the time, Pallas kernels for 0%

commit v1 on v0

--- a/solution.py
+++ b/solution.py
@@ -179,7 +179,7 @@
     basis = dir_terms + res_terms
     stacked = jnp.stack([term.reshape(-1) for term in basis])
     partial_gram = jnp.dot(stacked, stacked.T, precision=lax.Precision.HIGHEST)
-    gram = lax.psum(partial_gram, ("gx", "gy", "gz"))
+    gram = lax.psum(lax.psum(partial_gram, ("gy", "gz")), "gx")
     moved, residue, direct = coefficients(gram, center, half_width, STEPS)
     return (solution_in + combine(moved, basis), combine(residue, basis), combine(direct, basis))
 

time: 262 us -> 259 us (0.989)
    psum x1 -> x2, blocking collectives: 38.1 us -> 35.8 us  [body(): gram = lax.psum(lax.psum(partial_gram, ('gy', 'gz')), 'gx')]
where the time goes in v1:
time: 259 us; the launch traced here: 258 us
  waiting for transfers between devices  61 us (24%)
  starting transfers between devices  48.9 us (19%)
  other arithmetic  43.7 us (17%)
  local copies, waits for them, and re-layouts  42.5 us (16%)
  blocking collectives  35.8 us (14%)
  between operations  16 us (6%)
  matrix products  9.93 us (4%)
    ppermute x12, waiting for transfers between devices, extended(): lax.ppermute(lax.slice_in_dim(block, 0, width, axis=dim), axis, backward)  38.9 us
    psum x2, blocking collectives, body(): gram = lax.psum(lax.psum(partial_gram, ('gy', 'gz')), 'gx')  35.8 us
    ppermute x12, starting transfers between devices, extended(): lax.ppermute(lax.slice_in_dim(block, block.shape[dim] - width, None, axis...  27.1 us
    gather x1, local copies, waits for them, and re-layouts, body(): incoming = jnp.take_along_axis(arrived, slot, axis=1)  25.6 us
    ppermute x12, waiting for transfers between devices, extended(): lax.ppermute(lax.slice_in_dim(block, block.shape[dim] - width, None, axis...  18.2 us
    ppermute x12, starting transfers between devices, extended(): lax.ppermute(lax.slice_in_dim(block, 0, width, axis=dim), axis, backward)  15.5 us
    add x2, other arithmetic, combine(): summed = summed + weights[position] * basis[position]  12.8 us
    mul x5, other arithmetic, operate(): result = capacity * values  7.04 us
  transfers between devices with their start and end apart: 25, of which 18 were waited for; matrix products, arithmetic and copies ran while one was open for 5% of the time, Pallas kernels for 0%

profile of v1, /device:TPU:0, one launch (start us, length us, event | category | flops | bytes accessed | tf_op | source)
XLA Modules:
  0.0 257.8 jit_solution(11244546696564984081)
XLA Ops:
  2.2 6.3 %all-to-all-start = ((f32[4,1,1024]{2,1,0:T(1,128)}), f32[4,1,1024]{2,1,0:T(1,128)S(1)}, u32[]{:S(2)}, u32[]{:S(2)}) async-start(f32[4,1,1024]{2,1,0:T(1,128)} %reshape.745), calls=%async_computation | async-start | bytes 32768 | tf_op jit(solution)/shard_map/all_to_all | solution.py:140
  10.2 3.9 %all-to-all-done = f32[4,1,1024]{2,1,0:T(1,128)S(1)} async-done(((f32[4,1,1024]{2,1,0:T(1,128)}), f32[4,1,1024]{2,1,0:T(1,128)S(1)}, u32[]{:S(2)}, u32[]{:S(2)}) %all-to-all-start) | async-done | bytes 16416 | tf_op jit(solution)/shard_map/all_to_all | solution.py:140
  15.6 25.6 %gather_fusion = f32[4096]{0:T(1024)S(1)} fusion(f32[32,128]{1,0:T(8,128)S(1)} %reshape.660, s32[4096]{0:T(1024)S(1)} %fusion.80), kind=kCustom, calls=%fused_computation | custom fusion | bytes 65536 | tf_op jit(solution)/shard_map/jit(take_along_axis)/gather | solution.py:153
  41.3 3.4 %collective-permute-start = (f32[3,1,32,128]{3,2,1,0:T(8,128)S(1)}, f32[3,1,32,128]{3,2,1,0:T(8,128)S(1)}, u32[]{:S(2)}, u32[]{:S(2)}) collective-permute-start(f32[3,1,32,128]{3,2,1,0:T(8,128)S(1)} %get-tuple-element.320), channel_id=1, source_target_pairs={{0,16},{1,17},{2,18},{3,19},{4,20},{5,21},{6,22},{7,23},{8,24},{9,... | collective-permute-start | bytes 147464 | tf_op jit(solution)/shard_map/ppermute | solution.py:14
  46.7 4.0 %collective-permute-done.1 = f32[3,1,32,128]{3,2,1,0:T(8,128)S(1)} collective-permute-done((f32[3,1,32,128]{3,2,1,0:T(8,128)S(1)}, f32[3,1,32,128]{3,2,1,0:T(8,128)S(1)}, u32[]{:S(2)}, u32[]{:S(2)}) %collective-permute-start.1) | collective-permute-done | bytes 49184 | tf_op jit(solution)/shard_map/ppermute | solution.py:17
  54.0 2.8 %collective-permute-done.3 = f32[3,10,1,128]{3,2,1,0:T(1,128)S(1)} collective-permute-done((f32[3,10,1,128]{3,2,1,0:T(1,128)S(1)}, f32[3,10,1,128]{3,2,1,0:T(1,128)S(1)}, u32[]{:S(2)}, u32[]{:S(2)}) %collective-permute-start.3) | collective-permute-done | bytes 15392 | tf_op jit(solution)/shard_map/ppermute | solution.py:17
  67.0 5.8 %bitcast_multiply_fusion.6 = (f32[10,34,130]{2,1,0:T(8,128)S(1)}, f32[1,10,34,130]{3,2,1,0:T(8,128)S(1)}, pred[1,10,34,130]{3,2,1,0:T(8,128)(4,1)S(1)}, pred[1,1...) fusion(f32[3,10,34,130]{3,2,1,0:T(8,128)S(1)} %pad_maximum_fusi, ...), kind=kLoop, calls=%fused_computation.85 | loop fusion | flops 1060800 | bytes 1060832 | tf_op jit(solution)/shard_map/mul | solution.py:40
  72.8 5.4 %add_add_fusion = f32[1,10,34,130]{3,2,1,0:T(8,128)S(1)} fusion(pred[1,10,34,130]{3,2,1,0:T(8,128)(4,1)S(1)} %get-tuple-element.283, pred[1,10,34,130]{3,2,1,0:T(8,128)(4,1)S(1)} %get-tuple-element.282, pred[1,10,34,130]{3,2,1,0:T(8,128)(4,1)S(1)} %get-tuple-element.281, pred[1,10,34,130]{3,2,1,0:T(8,128)(4,1)S(1)} %get-tuple-element.280, ...), kind=kLoop, calls=%fused_computation.86 | loop fusion | flops 663000 | bytes 530432 | tf_op jit(solution)/shard_map/add | solution.py:65
  82.9 4.2 %collective-permute-done.7 = f32[2,1,32,128]{3,2,1,0:T(8,128)S(1)} collective-permute-done((f32[2,1,32,128]{3,2,1,0:T(8,128)S(1)}, f32[2,1,32,128]{3,2,1,0:T(8,128)S(1)}, u32[]{:S(2)}, u32[]{:S(2)}) %collective-permute-start.7) | collective-permute-done | bytes 32800 | tf_op jit(solution)/shard_map/ppermute | solution.py:17
  91.0 3.2 %collective-permute-done.9 = f32[2,10,1,128]{3,2,1,0:T(1,128)S(1)} collective-permute-done((f32[2,10,1,128]{3,2,1,0:T(1,128)S(1)}, f32[2,10,1,128]{3,2,1,0:T(1,128)S(1)}, u32[]{:S(2)}, u32[]{:S(2)}) %collective-permute-start.9) | collective-permute-done | bytes 10272 | tf_op jit(solution)/shard_map/ppermute | solution.py:17
  94.4 4.4 %collective-permute-start.10 = (f32[2,10,34,1]{3,2,1,0:T(8,128)S(1)}, f32[2,10,34,1]{3,2,1,0:T(8,128)S(1)}, u32[]{:S(2)}, u32[]{:S(2)}) collective-permute-start(f32[2,10,34,1]{3,2,1,0:T(8,128)S(1)} %get-tuple-element.318), channel_id=1, source_target_pairs={{0,1},{1,2},{2,3},{4,5},{5,6},{6,7},{8,9},{9,10},{10,11},{12,13},{... | collective-permute-start | bytes 8168 | tf_op jit(solution)/shard_map/ppermute | solution.py:14
  100.1 7.0 %collective-permute-done.10 = f32[2,10,34,1]{3,2,1,0:T(8,128)S(1)} collective-permute-done((f32[2,10,34,1]{3,2,1,0:T(8,128)S(1)}, f32[2,10,34,1]{3,2,1,0:T(8,128)S(1)}, u32[]{:S(2)}, u32[]{:S(2)}) %collective-permute-start.10) | collective-permute-done | bytes 2752 | tf_op jit(solution)/shard_map/ppermute | solution.py:14
  107.1 4.7 %collective-permute-done.11 = f32[2,10,34,1]{3,2,1,0:T(8,128)S(1)} collective-permute-done((f32[2,10,34,1]{3,2,1,0:T(8,128)S(1)}, f32[2,10,34,1]{3,2,1,0:T(8,128)S(1)}, u32[]{:S(2)}, u32[]{:S(2)}) %collective-permute-start.11) | collective-permute-done | bytes 2752 | tf_op jit(solution)/shard_map/ppermute | solution.py:17
  116.9 4.2 %collective-permute-done.13 = f32[2,1,32,128]{3,2,1,0:T(8,128)S(1)} collective-permute-done((f32[2,1,32,128]{3,2,1,0:T(8,128)S(1)}, f32[2,1,32,128]{3,2,1,0:T(8,128)S(1)}, u32[]{:S(2)}, u32[]{:S(2)}) %collective-permute-start.13) | collective-permute-done | bytes 32800 | tf_op jit(solution)/shard_map/ppermute | solution.py:17
  130.1 7.0 %collective-permute-done.16 = f32[2,10,34,1]{3,2,1,0:T(8,128)S(1)} collective-permute-done((f32[2,10,34,1]{3,2,1,0:T(8,128)S(1)}, f32[2,10,34,1]{3,2,1,0:T(8,128)S(1)}, u32[]{:S(2)}, u32[]{:S(2)}) %collective-permute-start.16) | collective-permute-done | bytes 2752 | tf_op jit(solution)/shard_map/ppermute | solution.py:14
  137.1 4.7 %collective-permute-done.17 = f32[2,10,34,1]{3,2,1,0:T(8,128)S(1)} collective-permute-done((f32[2,10,34,1]{3,2,1,0:T(8,128)S(1)}, f32[2,10,34,1]{3,2,1,0:T(8,128)S(1)}, u32[]{:S(2)}, u32[]{:S(2)}) %collective-permute-start.17) | collective-permute-done | bytes 2752 | tf_op jit(solution)/shard_map/ppermute | solution.py:17
  147.6 4.2 %collective-permute-done.19 = f32[1,32,128]{2,1,0:T(8,128)S(1)} collective-permute-done((f32[1,32,128]{2,1,0:T(8,128)S(1)}, f32[1,32,128]{2,1,0:T(8,128)S(1)}, u32[]{:S(2)}, u32[]{:S(2)}) %collective-permute-start.19) | collective-permute-done | bytes 16416 | tf_op jit(solution)/shard_map/ppermute | solution.py:17
  167.2 3.3 %collective-permute-done.22 = f32[10,34,1]{2,1,0:T(8,128)S(1)} collective-permute-done((f32[10,34,1]{2,1,0:T(8,128)S(1)}, f32[10,34,1]{2,1,0:T(8,128)S(1)}, u32[]{:S(2)}, u32[]{:S(2)}) %collective-permute-start.22) | collective-permute-done | bytes 1392 | tf_op jit(solution)/shard_map/ppermute | solution.py:14
  170.5 4.7 %collective-permute-done.23 = f32[10,34,1]{2,1,0:T(8,128)S(1)} collective-permute-done((f32[10,34,1]{2,1,0:T(8,128)S(1)}, f32[10,34,1]{2,1,0:T(8,128)S(1)}, u32[]{:S(2)}, u32[]{:S(2)}) %collective-permute-start.23) | collective-permute-done | bytes 1392 | tf_op jit(solution)/shard_map/ppermute | solution.py:17
  183.0 30.8 %psum.14 = f32[9,9]{1,0:T(8,128)S(1)} all-reduce(f32[9,9]{1,0:T(8,128)S(1)} %fusion.119), channel_id=1, replica_groups=mesh['gx'=2,'gy'=4,'gz'=4] {'gy','gz'}, use_global_device_ids=true, to_apply=%region_3.4 | all-reduce | flops 81 | bytes 648 | tf_op jit(solution)/shard_map/psum | solution.py:182
  213.8 5.0 %psum.15 = f32[9,9]{1,0:T(8,128)S(1)} all-reduce(f32[9,9]{1,0:T(8,128)S(1)} %psum.14), channel_id=1, replica_groups=mesh['gx'=2,'gy'=4,'gz'=4] {'gx'}, use_global_device_ids=true, to_apply=%region_4.5 | all-reduce | flops 81 | bytes 648 | tf_op jit(solution)/shard_map/psum | solution.py:182
  238.7 6.4 %multiply_add_fusion = f32[8,32,128]{2,1,0:T(8,128)} fusion(f32[8,32,128]{2,1,0:T(8,128)S(1)} %fusion.54, f32[8,32,128]{2,1,0:T(8,128)S(1)} %fusion.66, f32[8,32,128]{2,1,0:T(8,128)S(1)} %get-tuple-element.383, f32[8,32,128]{2,1,0:T(8,128)S(1)} %fusion.78, f32[8,32,128]{2,1,0:T(8,128)S(1)} %fusion.58, f32[8,32,128]{2,1,0:T(8,128)S(1)} %fusion.62, ...), kind=kLoop, calls=%fused_computation.187 | loop fusion | flops 557056 | bytes 1310756 | tf_op jit(solution)/shard_map/add | solution.py:126
  245.0 6.5 %multiply_add_fusion.1 = f32[8,32,128]{2,1,0:T(8,128)} fusion(f32[8,32,128]{2,1,0:T(8,128)S(1)} %fusion.54, f32[8,32,128]{2,1,0:T(8,128)S(1)} %fusion.66, f32[8,32,128]{2,1,0:T(8,128)S(1)} %get-tuple-element.383, f32[8,32,128]{2,1,0:T(8,128)S(1)} %fusion.78, f32[8,32,128]{2,1,0:T(8,128)S(1)} %fusion.58, f32[8,32,128]{2,1,0:T(8,128)S(1)} %fusion.62, ...), kind=kLoop, calls=%fused_computation.188 | loop fusion | flops 557056 | bytes 1310756 | tf_op jit(solution)/shard_map/add | solution.py:126
  251.5 6.3 %add_add_fusion.2 = f32[8,32,128]{2,1,0:T(8,128)} fusion(f32[8,32,128]{2,1,0:T(8,128)S(1)} %copy-done.3, f32[8,32,128]{2,1,0:T(8,128)S(1)} %fusion.54, f32[8,32,128]{2,1,0:T(8,128)S(1)} %fusion.66, f32[8,32,128]{2,1,0:T(8,128)S(1)} %get-tuple-element.383, f32[8,32,128]{2,1,0:T(8,128)S(1)} %fusion.78, f32[8,32,128]{2,1,0:T(8,128)S(1)} %fusion.58, ...), kind=kLoop, calls=%fused_computation.189 | loop fusion | flops 589824 | bytes 1441828 | tf_op jit(solution)/shard_map/add | solution.py:184
  (170 shorter events, 77.9 us)
Async XLA Ops:
  2.2 11.9 %all-to-all-start = ((f32[4,1,1024]{2,1,0:T(1,128)}), f32[4,1,1024]{2,1,0:T(1,128)S(1)}, u32[]{:S(2)}, u32[]{:S(2)}) async-start(f32[4,1,1024]{2,1,0:T(1,128)} %reshape.745), calls=%async_computation | async-start | bytes 32768 | tf_op jit(solution)/shard_map/all_to_all | solution.py:140
  41.3 5.4 %collective-permute-start = (f32[3,1,32,128]{3,2,1,0:T(8,128)S(1)}, f32[3,1,32,128]{3,2,1,0:T(8,128)S(1)}, u32[]{:S(2)}, u32[]{:S(2)}) collective-permute-start(f32[3,1,32,128]{3,2,1,0:T(8,128)S(1)} %get-tuple-element.320), channel_id=1, source_target_pairs={{0,16},{1,17},{2,18},{3,19},{4,20},{5,21},{6,22},{7,23},{8,24},{9,... | collective-permute-start | bytes 147464 | tf_op jit(solution)/shard_map/ppermute | solution.py:14
  44.7 6.0 %collective-permute-start.1 = (f32[3,1,32,128]{3,2,1,0:T(8,128)S(1)}, f32[3,1,32,128]{3,2,1,0:T(8,128)S(1)}, u32[]{:S(2)}, u32[]{:S(2)}) collective-permute-start(f32[3,1,32,128]{3,2,1,0:T(8,128)S(1)} %get-tuple-element.321), channel_id=1, source_target_pairs={{16,0},{17,1},{18,2},{19,3},{20,4},{21,5},{22,6},{23,7},{24,8},{25... | collective-permute-start | bytes 147464 | tf_op jit(solution)/shard_map/ppermute | solution.py:17
  50.7 3.3 %collective-permute-start.2 = (f32[3,10,1,128]{3,2,1,0:T(1,128)S(1)}, f32[3,10,1,128]{3,2,1,0:T(1,128)S(1)}, u32[]{:S(2)}, u32[]{:S(2)}) collective-permute-start(f32[3,10,1,128]{3,2,1,0:T(1,128)S(1)} %get-tuple-element.306), channel_id=1, source_target_pairs={{0,4},{4,8},{8,12},{1,5},{5,9},{9,13},{2,6},{6,10},{10,14},{3,7},{... | collective-permute-start | bytes 46088 | tf_op jit(solution)/shard_map/ppermute | solution.py:14
  52.0 4.8 %collective-permute-start.3 = (f32[3,10,1,128]{3,2,1,0:T(1,128)S(1)}, f32[3,10,1,128]{3,2,1,0:T(1,128)S(1)}, u32[]{:S(2)}, u32[]{:S(2)}) collective-permute-start(f32[3,10,1,128]{3,2,1,0:T(1,128)S(1)} %get-tuple-element.307), channel_id=1, source_target_pairs={{4,0},{8,4},{12,8},{5,1},{9,5},{13,9},{6,2},{10,6},{14,10},{7,3},{... | collective-permute-start | bytes 46088 | tf_op jit(solution)/shard_map/ppermute | solution.py:17
  57.4 7.9 %collective-permute-start.4 = (f32[3,10,34,1]{2,3,1,0:T(1,128)S(1)}, f32[3,10,34,1]{2,3,1,0:T(1,128)S(1)}, u32[]{:S(2)}, u32[]{:S(2)}) collective-permute-start(f32[3,10,34,1]{2,3,1,0:T(1,128)S(1)} %copy.31), channel_id=1, source_target_pairs={{0,1},{1,2},{2,3},{4,5},{5,6},{6,7},{8,9},{9,10},{10,11},{12,13},{... | collective-permute-start | bytes 12248 | tf_op jit(solution)/shard_map/ppermute | solution.py:14
  60.3 5.6 %collective-permute-start.5 = (f32[3,10,34,1]{2,3,1,0:T(1,128)S(1)}, f32[3,10,34,1]{2,3,1,0:T(1,128)S(1)}, u32[]{:S(2)}, u32[]{:S(2)}) collective-permute-start(f32[3,10,34,1]{2,3,1,0:T(1,128)S(1)} %copy.32), channel_id=1, source_target_pairs={{1,0},{2,1},{3,2},{5,4},{6,5},{7,6},{9,8},{10,9},{11,10},{13,12},{... | collective-permute-start | bytes 12248 | tf_op jit(solution)/shard_map/ppermute | solution.py:17
  79.7 3.2 %collective-permute-start.6 = (f32[2,1,32,128]{3,2,1,0:T(8,128)S(1)}, f32[2,1,32,128]{3,2,1,0:T(8,128)S(1)}, u32[]{:S(2)}, u32[]{:S(2)}) collective-permute-start(f32[2,1,32,128]{3,2,1,0:T(8,128)S(1)} %get-tuple-element.328), channel_id=1, source_target_pairs={{0,16},{1,17},{2,18},{3,19},{4,20},{5,21},{6,22},{7,23},{8,24},{9,... | collective-permute-start | bytes 98312 | tf_op jit(solution)/shard_map/ppermute | solution.py:14
  81.3 5.8 %collective-permute-start.7 = (f32[2,1,32,128]{3,2,1,0:T(8,128)S(1)}, f32[2,1,32,128]{3,2,1,0:T(8,128)S(1)}, u32[]{:S(2)}, u32[]{:S(2)}) collective-permute-start(f32[2,1,32,128]{3,2,1,0:T(8,128)S(1)} %get-tuple-element.329), channel_id=1, source_target_pairs={{16,0},{17,1},{18,2},{19,3},{20,4},{21,5},{22,6},{23,7},{24,8},{25... | collective-permute-start | bytes 98312 | tf_op jit(solution)/shard_map/ppermute | solution.py:17
  87.2 3.8 %collective-permute-start.8 = (f32[2,10,1,128]{3,2,1,0:T(1,128)S(1)}, f32[2,10,1,128]{3,2,1,0:T(1,128)S(1)}, u32[]{:S(2)}, u32[]{:S(2)}) collective-permute-start(f32[2,10,1,128]{3,2,1,0:T(1,128)S(1)} %get-tuple-element.324), channel_id=1, source_target_pairs={{0,4},{4,8},{8,12},{1,5},{5,9},{9,13},{2,6},{6,10},{10,14},{3,7},{... | collective-permute-start | bytes 30728 | tf_op jit(solution)/shard_map/ppermute | solution.py:14
  89.6 4.5 %collective-permute-start.9 = (f32[2,10,1,128]{3,2,1,0:T(1,128)S(1)}, f32[2,10,1,128]{3,2,1,0:T(1,128)S(1)}, u32[]{:S(2)}, u32[]{:S(2)}) collective-permute-start(f32[2,10,1,128]{3,2,1,0:T(1,128)S(1)} %get-tuple-element.325), channel_id=1, source_target_pairs={{4,0},{8,4},{12,8},{5,1},{9,5},{13,9},{6,2},{10,6},{14,10},{7,3},{... | collective-permute-start | bytes 30728 | tf_op jit(solution)/shard_map/ppermute | solution.py:17
  94.4 12.7 %collective-permute-start.10 = (f32[2,10,34,1]{3,2,1,0:T(8,128)S(1)}, f32[2,10,34,1]{3,2,1,0:T(8,128)S(1)}, u32[]{:S(2)}, u32[]{:S(2)}) collective-permute-start(f32[2,10,34,1]{3,2,1,0:T(8,128)S(1)} %get-tuple-element.318), channel_id=1, source_target_pairs={{0,1},{1,2},{2,3},{4,5},{5,6},{6,7},{8,9},{9,10},{10,11},{12,13},{... | collective-permute-start | bytes 8168 | tf_op jit(solution)/shard_map/ppermute | solution.py:14
  98.8 13.0 %collective-permute-start.11 = (f32[2,10,34,1]{3,2,1,0:T(8,128)S(1)}, f32[2,10,34,1]{3,2,1,0:T(8,128)S(1)}, u32[]{:S(2)}, u32[]{:S(2)}) collective-permute-start(f32[2,10,34,1]{3,2,1,0:T(8,128)S(1)} %get-tuple-element.319), channel_id=1, source_target_pairs={{1,0},{2,1},{3,2},{5,4},{6,5},{7,6},{9,8},{10,9},{11,10},{13,12},{... | collective-permute-start | bytes 8168 | tf_op jit(solution)/shard_map/ppermute | solution.py:17
  113.6 3.3 %collective-permute-start.12 = (f32[2,1,32,128]{3,2,1,0:T(8,128)S(1)}, f32[2,1,32,128]{3,2,1,0:T(8,128)S(1)}, u32[]{:S(2)}, u32[]{:S(2)}) collective-permute-start(f32[2,1,32,128]{3,2,1,0:T(8,128)S(1)} %get-tuple-element.326), channel_id=1, source_target_pairs={{0,16},{1,17},{2,18},{3,19},{4,20},{5,21},{6,22},{7,23},{8,24},{9,... | collective-permute-start | bytes 98312 | tf_op jit(solution)/shard_map/ppermute | solution.py:14
  115.2 5.9 %collective-permute-start.13 = (f32[2,1,32,128]{3,2,1,0:T(8,128)S(1)}, f32[2,1,32,128]{3,2,1,0:T(8,128)S(1)}, u32[]{:S(2)}, u32[]{:S(2)}) collective-permute-start(f32[2,1,32,128]{3,2,1,0:T(8,128)S(1)} %get-tuple-element.327), channel_id=1, source_target_pairs={{16,0},{17,1},{18,2},{19,3},{20,4},{21,5},{22,6},{23,7},{24,8},{25... | collective-permute-start | bytes 98312 | tf_op jit(solution)/shard_map/ppermute | solution.py:17
  121.1 3.1 %collective-permute-start.14 = (f32[2,10,1,128]{3,2,1,0:T(1,128)S(1)}, f32[2,10,1,128]{3,2,1,0:T(1,128)S(1)}, u32[]{:S(2)}, u32[]{:S(2)}) collective-permute-start(f32[2,10,1,128]{3,2,1,0:T(1,128)S(1)} %get-tuple-element.322), channel_id=1, source_target_pairs={{0,4},{4,8},{8,12},{1,5},{5,9},{9,13},{2,6},{6,10},{10,14},{3,7},{... | collective-permute-start | bytes 30728 | tf_op jit(solution)/shard_map/ppermute | solution.py:14
  122.9 3.2 %collective-permute-start.15 = (f32[2,10,1,128]{3,2,1,0:T(1,128)S(1)}, f32[2,10,1,128]{3,2,1,0:T(1,128)S(1)}, u32[]{:S(2)}, u32[]{:S(2)}) collective-permute-start(f32[2,10,1,128]{3,2,1,0:T(1,128)S(1)} %get-tuple-element.323), channel_id=1, source_target_pairs={{4,0},{8,4},{12,8},{5,1},{9,5},{13,9},{6,2},{10,6},{14,10},{7,3},{... | collective-permute-start | bytes 30728 | tf_op jit(solution)/shard_map/ppermute | solution.py:17
  126.4 10.7 %collective-permute-start.16 = (f32[2,10,34,1]{3,2,1,0:T(8,128)S(1)}, f32[2,10,34,1]{3,2,1,0:T(8,128)S(1)}, u32[]{:S(2)}, u32[]{:S(2)}) collective-permute-start(f32[2,10,34,1]{3,2,1,0:T(8,128)S(1)} %get-tuple-element.312), channel_id=1, source_target_pairs={{0,1},{1,2},{2,3},{4,5},{5,6},{6,7},{8,9},{9,10},{10,11},{12,13},{... | collective-permute-start | bytes 8168 | tf_op jit(solution)/shard_map/ppermute | solution.py:14
  128.8 13.0 %collective-permute-start.17 = (f32[2,10,34,1]{3,2,1,0:T(8,128)S(1)}, f32[2,10,34,1]{3,2,1,0:T(8,128)S(1)}, u32[]{:S(2)}, u32[]{:S(2)}) collective-permute-start(f32[2,10,34,1]{3,2,1,0:T(8,128)S(1)} %get-tuple-element.313), channel_id=1, source_target_pairs={{1,0},{2,1},{3,2},{5,4},{6,5},{7,6},{9,8},{10,9},{11,10},{13,12},{... | collective-permute-start | bytes 8168 | tf_op jit(solution)/shard_map/ppermute | solution.py:17
  146.2 5.6 %collective-permute-start.19 = (f32[1,32,128]{2,1,0:T(8,128)S(1)}, f32[1,32,128]{2,1,0:T(8,128)S(1)}, u32[]{:S(2)}, u32[]{:S(2)}) collective-permute-start(f32[1,32,128]{2,1,0:T(8,128)S(1)} %get-tuple-element.335), channel_id=1, source_target_pairs={{16,0},{17,1},{18,2},{19,3},{20,4},{21,5},{22,6},{23,7},{24,8},{25... | collective-permute-start | bytes 49160 | tf_op jit(solution)/shard_map/ppermute | solution.py:17
  151.9 11.3 %collective-permute-start.20 = (f32[10,1,128]{2,1,0:T(1,128)S(1)}, f32[10,1,128]{2,1,0:T(1,128)S(1)}, u32[]{:S(2)}, u32[]{:S(2)}) collective-permute-start(f32[10,1,128]{2,1,0:T(1,128)S(1)} %get-tuple-element.332), channel_id=1, source_target_pairs={{0,4},{4,8},{8,12},{1,5},{5,9},{9,13},{2,6},{6,10},{10,14},{3,7},{... | collective-permute-start | bytes 15368 | tf_op jit(solution)/shard_map/ppermute | solution.py:14
  153.4 9.8 %collective-permute-start.21 = (f32[10,1,128]{2,1,0:T(1,128)S(1)}, f32[10,1,128]{2,1,0:T(1,128)S(1)}, u32[]{:S(2)}, u32[]{:S(2)}) collective-permute-start(f32[10,1,128]{2,1,0:T(1,128)S(1)} %get-tuple-element.333), channel_id=1, source_target_pairs={{4,0},{8,4},{12,8},{5,1},{9,5},{13,9},{6,2},{10,6},{14,10},{7,3},{... | collective-permute-start | bytes 15368 | tf_op jit(solution)/shard_map/ppermute | solution.py:17
  163.3 7.2 %collective-permute-start.22 = (f32[10,34,1]{2,1,0:T(8,128)S(1)}, f32[10,34,1]{2,1,0:T(8,128)S(1)}, u32[]{:S(2)}, u32[]{:S(2)}) collective-permute-start(f32[10,34,1]{2,1,0:T(8,128)S(1)} %get-tuple-element.330), channel_id=1, source_target_pairs={{0,1},{1,2},{2,3},{4,5},{5,6},{6,7},{8,9},{9,10},{10,11},{12,13},{... | collective-permute-start | bytes 4088 | tf_op jit(solution)/shard_map/ppermute | solution.py:14
  165.8 9.5 %collective-permute-start.23 = (f32[10,34,1]{2,1,0:T(8,128)S(1)}, f32[10,34,1]{2,1,0:T(8,128)S(1)}, u32[]{:S(2)}, u32[]{:S(2)}) collective-permute-start(f32[10,34,1]{2,1,0:T(8,128)S(1)} %get-tuple-element.331), channel_id=1, source_target_pairs={{1,0},{2,1},{3,2},{5,4},{6,5},{7,6},{9,8},{10,9},{11,10},{13,12},{... | collective-permute-start | bytes 4088 | tf_op jit(solution)/shard_map/ppermute | solution.py:17
  (12 other events, 302.1 us)
